TPU v7x, 1024 devices: a whole 4x8x16 slice. The times are simulated.
1024 devices in a mesh: ctx: 128 (over x, z, core), tp: 8 (over y).
Axes of the slice: x: 4, y: 8, z: 16, core: 2. Of those that a mesh axis runs over, the one named last changes fastest.
Arguments:
- streams: bfloat16 [3, 16384, 8192], P(None, 'ctx', 'tp'), may hold values from -6 to 6
- short_filter: bfloat16 [3, 512, 7], P(None, 'tp'), may hold values from -3 to 3
- decay_rate: float32 [16, 8192], P(None, 'tp'), may hold values from 1.8310548e-05 to 0.05
- residue: float32 [16, 8192], P(None, 'tp'), may hold values from -5 to 5
- norm_gain: float32 [8192], P('tp'), may hold values from 0.5 to 1.5
- out_grad: bfloat16 [16384, 8192], P('ctx', 'tp'), may hold values from -6 to 6
Outputs:
- output: bfloat16 [16384, 8192], P('ctx', 'tp')
- stream_grads: bfloat16 [3, 16384, 8192], P(None, 'ctx', 'tp')
All inputs are finite; a program needn't handle non-finite values.
Results may differ from a plain program's by a relative error of at most 0.002.
Values may be sent and summed in bfloat16 or wider, within the bound.
A program may use at most 64 MiB of HBM per device.

v0:
```python
import jax
import jax.numpy as jnp
from jax import lax
from jax.sharding import PartitionSpec as P

GROUP = 16
BLOCK = 16


EPSILON = 1e-05


def shifted(block, axis, distance):
    devices = range(lax.axis_size(axis))
    route = [(i - distance, i) for i in devices if i - distance in devices]
    return lax.ppermute(block, axis, route)


def carried_in(part, axis, combine, identity, reverse):
    count = lax.axis_size(axis)
    place = lax.axis_index(axis)
    ahead = count - 1 - place if reverse else place
    gathered = jax.tree.map(lambda a: lax.all_gather(a, axis), part)
    state = jax.tree.map(lambda a, e: jnp.zeros_like(a) + jnp.asarray(e, a.dtype), part, identity)

    def one(turn, state):
        source = count - 1 - turn if reverse else turn
        return combine(
            state, jax.tree.map(lambda a: lax.dynamic_index_in_dim(a, source, 0, False), gathered)
        )

    return lax.fori_loop(0, ahead, one, state)


def for_sending(value):
    return jax.tree.map(lambda a: a.astype(jnp.bfloat16) if a.dtype == jnp.float32 else a, value)


def channel_weights(short_filter):
    stream_count, group_count, tap_count = short_filter.shape
    spread = jnp.broadcast_to(
        short_filter.astype(jnp.float32)[:, :, None, :],
        (stream_count, group_count, GROUP, tap_count),
    )
    return jnp.transpose(spread.reshape(stream_count, group_count * GROUP, tap_count), (0, 2, 1))


def filter_tables(decay_rate, residue):
    lag_steps = jnp.arange(BLOCK, dtype=jnp.float32)
    scaled = residue * jnp.sqrt(2.0 * decay_rate)
    places = jnp.arange(BLOCK, dtype=jnp.int32)
    lagged = places[:, None] - places[None, :]
    lag_float = jnp.maximum(lagged, 0).astype(jnp.float32)
    terms = scaled[:, None, None, :] * jnp.exp(
        -decay_rate[:, None, None, :] * lag_float[None, :, :, None]
    )
    toeplitz = jnp.where(
        (lagged >= 0)[:, :, None], jnp.sum(terms, axis=0), jnp.zeros((), jnp.float32)
    )
    end_weight = jnp.exp(-decay_rate[:, None, :] * (BLOCK - 1.0 - lag_steps)[None, :, None])
    out_weight = scaled[:, None, :] * jnp.exp(
        -decay_rate[:, None, :] * (lag_steps + 1.0)[None, :, None]
    )
    return (toeplitz, end_weight, out_weight)


def block_terms(signal, tables):
    toeplitz, end_weight, out_weight = tables
    pieces = signal.reshape(-1, BLOCK, signal.shape[-1])
    within = jnp.sum(toeplitz[None, :, :, :] * pieces[:, None, :, :], axis=2)
    block_ends = jnp.sum(end_weight[None, :, :, :] * pieces[:, None, :, :], axis=2)
    return (within, block_ends)


def chain_blocks(block_ends, block_decay):

    def advance(carried_state, block_term):
        return (block_decay * carried_state + block_term, carried_state)

    zero_state = jnp.zeros(block_decay.shape, jnp.float32)
    return lax.scan(advance, zero_state, block_ends)


def apply_states(within, entering, incoming, decay_rate, out_weight):
    block_count = entering.shape[0]
    offsets = jnp.arange(block_count, dtype=jnp.float32) * BLOCK
    entering = (
        entering + jnp.exp(-decay_rate[None, :, :] * offsets[:, None, None]) * incoming[None, :, :]
    )
    carried = jnp.sum(out_weight[None, :, :, :] * entering[:, :, None, :], axis=1)
    return (within + carried).reshape(-1, within.shape[-1])


def scan_pieces(local_end, decay_rate, row_count):

    def combine(earlier_part, later_part):
        reach_decay = jnp.exp(-decay_rate * (row_count * later_part[0]))
        return (earlier_part[0] + later_part[0], reach_decay * earlier_part[1] + later_part[1])

    elements = (jnp.ones((), jnp.float32), local_end)
    identity = (jnp.zeros((), jnp.float32), jnp.zeros_like(local_end))
    return (elements, combine, identity)


def on_device(streams, short_filter, decay_rate, residue, norm_gain, out_grad):
    stream_count, row_count, channels = streams.shape
    reach_rows = short_filter.shape[2] - 1
    weights = channel_weights(short_filter)
    earlier_rows = shifted(streams[:, row_count - reach_rows :, :], "ctx", 1)
    extended = jnp.concatenate([earlier_rows, streams], axis=1)
    convolved = weights[:, 0, None, :] * extended[:, reach_rows:, :].astype(jnp.float32)
    for offset in range(1, reach_rows + 1):
        convolved = convolved + weights[:, offset, None, :] * extended[
            :, reach_rows - offset : reach_rows - offset + row_count, :
        ].astype(jnp.float32)
    query_conv = convolved[0]
    key_conv = convolved[1]
    value_conv = convolved[2]
    tables = filter_tables(decay_rate, residue)
    block_decay = jnp.exp(-decay_rate * BLOCK)
    within, block_ends = block_terms(key_conv * value_conv, tables)
    local_end, entering = chain_blocks(block_ends, block_decay)
    elements, combine, identity = scan_pieces(local_end, decay_rate, row_count)
    incoming = carried_in(elements, "ctx", combine, identity, False)[1]
    long_conv = apply_states(within, entering, incoming, decay_rate, tables[2])
    modulated = query_conv * long_conv
    scaled_grad = norm_gain * out_grad.astype(jnp.float32)
    square_sum, cross_sum = lax.psum(
        (jnp.sum(modulated * modulated, axis=1), jnp.sum(scaled_grad * modulated, axis=1)), "tp"
    )
    total_width = channels * lax.axis_size("tp")
    inverse = lax.rsqrt(square_sum / total_width + EPSILON)
    output = (norm_gain * modulated * inverse[:, None]).astype(jnp.bfloat16)
    mixed_grad = (
        inverse[:, None] * scaled_grad
        - modulated * (inverse * inverse * inverse * cross_sum / total_width)[:, None]
    )
    query_grad = mixed_grad * long_conv
    long_grad = mixed_grad * query_conv
    within_back, ends_back = block_terms(jnp.flip(long_grad, axis=0), tables)
    end_back, entering_back = chain_blocks(ends_back, block_decay)
    elements_back, combine_back, identity_back = scan_pieces(end_back, decay_rate, row_count)
    later_state = carried_in(elements_back, "ctx", combine_back, identity_back, True)[1]
    gated_grad = jnp.flip(
        apply_states(within_back, entering_back, later_state, decay_rate, tables[2]), axis=0
    )
    conv_grad = jnp.stack([query_grad, gated_grad * value_conv, gated_grad * key_conv])
    later_rows = shifted(for_sending(conv_grad[:, :reach_rows, :]), "ctx", -1)
    extended_grad = jnp.concatenate([conv_grad, later_rows], axis=1)
    summed = weights[:, 0, None, :] * conv_grad
    for offset in range(1, reach_rows + 1):
        summed = (
            summed + weights[:, offset, None, :] * extended_grad[:, offset : offset + row_count, :]
        )
    return (output, summed.astype(jnp.bfloat16))


def solution(mesh):
    return jax.shard_map(
        on_device,
        mesh=mesh,
        in_specs=(
            P(None, "ctx", "tp"),
            P(None, "tp", None),
            P(None, "tp"),
            P(None, "tp"),
            P("tp"),
            P("ctx", "tp"),
        ),
        out_specs=(P("ctx", "tp"), P(None, "ctx", "tp")),
        check_vma=False,
    )
```

profile of v0, /device:TPU:1, one launch (start us, length us, event | category | flops | bytes accessed | tf_op | source)
XLA Modules:
  0.0 1046.9 jit_solution(15421726308259993159)
XLA Ops:
  8.0 5.4 collective-permute-start
  13.5 0.9 broadcast_in_dim.20
  14.9 2.8 multiply_reduce_fusion
  17.7 1.7 exponential_multiply_fusion
  19.6 4.5 collective-permute-done
  24.2 4.2 multiply_add_fusion
  28.5 4.0 multiply_reduce_fusion.5
  33.3 12.2 %while.56 = (s32[]{:T(128)}, f32[16,1024]{1,0:T(8,128)S(1)}, f32[8,16,1024]{2,1,0:T(8,128)}, f32[16,1024]{1,0:T(8,128)S(1)}, f32[8,16,1024]{2,1,0:T(8,128)}, /*index=5*/s32[]{:T(128)}, s32[]{:T(128)}) while((s32[]{:T(128)}, f32[16,1024]{1,0:T(8,128)S(1)}, f32[8,16,1024]{2,1,0:T(8,128)}, f32[16,1024]{1,0:T(8,128)S(1)}, ...), condition=%wide.region_4.5_spmd.clone, body=%wide.region_3.4_spmd.clone.sunk | while | flops 65539 | bytes 393320 | solution.py:81
  46.2 1.3 dynamic-slice
  48.2 253.7 %all-reduce = f32[128]{0:T(128)S(1)} all-reduce(f32[128]{0:T(128)S(1)} %dynamic-update-slice), channel_id=1, replica_groups=mesh['ctx'=128,'tp'=8] {'ctx'}, use_global_device_ids=true, to_apply=%add | all-reduce | flops 128 | bytes 1024
  302.0 2.1 while.54
  303.2 0.9 bitcast_add_fusion.8
  304.1 1.3 multiply_add_fusion.2
  307.0 0.9 multiply_reduce_fusion.7
  307.9 14.1 %all-reduce.1 = (f32[128]{0:T(128)S(1)}, f32[128]{0:T(128)S(1)}) all-reduce(f32[128]{0:T(128)S(1)} %get-tuple-element.296, f32[128]{0:T(128)S(1)} %get-tuple-element.295), channel_id=1, replica_groups=mesh['ctx'=128,'tp'=8] {'tp'}, use_global_device_ids=true, to_apply=%region_9.10 | all-reduce | flops 256 | bytes 2048 | tf_op jit(solution)/shard_map/psum | solution.py:128
  322.0 2.4 bitcast_multiply_fusion.2
  324.3 4.7 rev.7
  329.1 6.3 multiply_reduce_fusion.2
  336.3 12.2 %while.57 = (s32[]{:T(128)}, f32[16,1024]{1,0:T(8,128)S(1)}, f32[8,16,1024]{2,1,0:T(8,128)}, f32[16,1024]{1,0:T(8,128)S(1)}, f32[8,16,1024]{2,1,0:T(8,128)}, /*index=5*/s32[]{:T(128)}, s32[]{:T(128)}) while((s32[]{:T(128)}, f32[16,1024]{1,0:T(8,128)S(1)}, f32[8,16,1024]{2,1,0:T(8,128)}, f32[16,1024]{1,0:T(8,128)S(1)}, ...), condition=%wide.region_15.16_spmd.clone, body=%wide.region_14.15_spmd.clone.sunk | while | flops 65539 | bytes 393320 | solution.py:81
  349.1 412.7 %all-gather.7.cloned.1.call-done = f32[2048,1024]{1,0:T(8,128)} async-done(((f32[16,1024]{1,0:T(8,128)}), f32[2048,1024]{1,0:T(8,128)}) %all-gather.7.cloned.1.call-update) | async-done | bytes 8388624 | tf_op jit(solution)/shard_map/all_gather | solution.py:23
  761.8 268.0 %while.55 = (s32[]{:T(128)}, f32[16,1024]{1,0:T(8,128)S(1)}, s32[]{:T(128)}, f32[128]{0:T(128)S(1)}, f32[16,1024]{1,0:T(8,128)S(1)}, /*index=5*/f32[128,16,1024]...) while((s32[]{:T(128)}, f32[16,1024]{1,0:T(8,128)S(1)}, s32[]{:T(128)}, ...), condition=%wide.region_17.18_spmd, body=%wide.region_16.17_spmd.sunk | while | flops 49159 | bytes 262339 | solution.py:32
  763.0 0.9 bitcast_add_fusion.9
  773.7 0.9 bitcast_add_fusion.9
  777.9 0.9 bitcast_add_fusion.9
  784.3 0.9 bitcast_add_fusion.9
  788.6 0.9 bitcast_add_fusion.9
  792.8 0.9 bitcast_add_fusion.9
  799.2 0.9 bitcast_add_fusion.9
  803.5 0.9 bitcast_add_fusion.9
  814.1 0.9 bitcast_add_fusion.9
  818.3 0.9 bitcast_add_fusion.9
  824.7 0.9 bitcast_add_fusion.9
  829.0 0.9 bitcast_add_fusion.9
  833.2 0.9 bitcast_add_fusion.9
  839.6 0.9 bitcast_add_fusion.9
  843.9 0.9 bitcast_add_fusion.9
  854.5 0.9 bitcast_add_fusion.9
  858.8 0.9 bitcast_add_fusion.9
  865.2 0.9 bitcast_add_fusion.9
  869.4 0.9 bitcast_add_fusion.9
  873.7 0.9 bitcast_add_fusion.9
  880.0 0.9 bitcast_add_fusion.9
  884.3 0.9 bitcast_add_fusion.9
  894.9 0.9 bitcast_add_fusion.9
  899.2 0.9 bitcast_add_fusion.9
  905.6 0.9 bitcast_add_fusion.9
  909.8 0.9 bitcast_add_fusion.9
  914.1 0.9 bitcast_add_fusion.9
  920.5 0.9 bitcast_add_fusion.9
  924.7 0.9 bitcast_add_fusion.9
  935.4 0.9 bitcast_add_fusion.9
  939.6 0.9 bitcast_add_fusion.9
  946.0 0.9 bitcast_add_fusion.9
  950.2 0.9 bitcast_add_fusion.9
  954.5 0.9 bitcast_add_fusion.9
  960.9 0.9 bitcast_add_fusion.9
  965.1 0.9 bitcast_add_fusion.9
  975.8 0.9 bitcast_add_fusion.9
  980.0 0.9 bitcast_add_fusion.9
  986.4 0.9 bitcast_add_fusion.9
  1029.9 1.3 multiply_add_fusion.1
  1032.3 4.3 collective-permute-start.1
  1036.7 1.1 collective-permute-done.1
  1037.9 2.2 fusion.1
  (306 shorter events, 184.7 us)
Async XLA Ops:
  7.2 7.7 copy-start.8
  7.2 7.7 copy-start.9
  7.2 294.8 %all-gather.5.cloned.1.call-start = ((), (), s32[]{:S(2)}) async-start(), calls=%async_computation | async-start | bytes 8454144 | tf_op jit(solution)/shard_map/all_gather | solution.py:23
  8.0 16.1 %collective-permute-start = (bf16[3,6,1024]{2,1,0:T(8,128)(2,1)S(1)}, bf16[3,6,1024]{2,1,0:T(8,128)(2,1)S(1)}, u32[]{:S(2)}, u32[]{:S(2)}) collective-permute-start(bf16[3,6,1024]{2,1,0:T(8,128)(2,1)S(1)} %slice.82), channel_id=1, source_target_pairs={{0,8},{8,16},{16,24},{24,32},{32,40},{40,48},{48,56},{56,64},{64,7... | collective-permute-start | bytes 110600 | tf_op jit(solution)/shard_map/ppermute | solution.py:16
  24.2 4.3 copy-start
  45.5 0.6 copy-start.4
  46.1 715.7 %all-gather.7.cloned.1.call-start = ((), (), s32[]{:S(2)}) async-start(), calls=%async_computation.1 | async-start | bytes 8454144 | tf_op jit(solution)/shard_map/all_gather | solution.py:23
  304.1 1.4 copy-start.1
  305.5 1.5 copy-start.7
  305.5 1.5 copy-start.10
  306.2 0.8 copy-start.5
  348.5 0.6 copy-start.3
  348.5 682.6 %copy-start.2 = (f32[16,16,1024]{2,1,0:T(8,128)S(1)}, f32[16,16,1024]{2,1,0:T(8,128)}, u32[]{:S(2)}) copy-start(f32[16,16,1024]{2,1,0:T(8,128)} %get-tuple-element.358) | copy-start | bytes 3145732
  1029.8 1.9 copy-start.6
  1032.3 5.4 collective-permute-start.1
Sparse Core Ops, SparseCore 0:
  46.2 156.1 all-gather.4
  349.3 412.5 all-gather.6
where the time goes:
time: 1060 us; the launch traced here: 1050 us
  waiting for transfers between devices  418 us (39%)
  blocking collectives  268 us (25%)
  other arithmetic  165 us (16%)
  local copies, waits for them, and re-layouts  88.9 us (8%)
  loops' own time  83 us (8%)
  between operations  14.4 us (1%)
    all_gather x2, waiting for transfers between devices, carried_in(): gathered = jax.tree.map(lambda a: lax.all_gather(a, axis), part)  413 us
    unnamed x1, blocking collectives  254 us
    add x127, other arithmetic, combine(): reach_decay * earlier_part[1] + later_part[1]  112 us
    another operation x2, loops' own time, carried_in(): return lax.fori_loop(0, ahead, one, state)  82.7 us
    dynamic_slice x127, local copies, waits for them, and re-layouts, one(): lax.dynamic_index_in_dim(a, source, 0, False)  75.9 us
  transfers between devices with their start and end apart: 4, of which 3 were waited for; matrix products, arithmetic and copies ran while one was open for 1% of the time, Pallas kernels for 0%

commit v1 on v0

v1 whole, which is shorter than its diff:
```python
import functools

import jax
import jax.numpy as jnp
from jax import lax
from jax.experimental import pallas as pl
from jax.experimental.pallas import tpu as pltpu
from jax.sharding import PartitionSpec as P

MESH = pl.DeviceIdType.MESH
F32 = jnp.float32
BF16 = jnp.bfloat16
GROUP = 16
EPSILON = 1e-05
ROWS = 128
EXT = 8
HALO = 8
TAPS = 7
MODES = 16
SUB = 8
LANES = 128
TILES = 8
ROW_DEVICES = 32
X_COUNT = 4
BLOCKS = (ROWS + EXT) // 8


def rows_of(ref, start, count):
    offset = start * SUB
    if not isinstance(offset, int):
        offset = pl.multiple_of(offset, SUB)
    return ref[pl.ds(offset, count * SUB), :].reshape(count, SUB, LANES)


def put_rows(ref, start, value):
    offset = start * SUB
    if not isinstance(offset, int):
        offset = pl.multiple_of(offset, SUB)
    ref[pl.ds(offset, value.shape[0] * SUB), :] = value.reshape(value.shape[0] * SUB, LANES)


def spread(ref, start, tile, value):
    ref[pl.ds(start * SUB + tile, value.shape[0], stride=SUB), :] = value


def gathered(ref, start, count, tile):
    return ref[pl.ds(start * SUB + tile, count, stride=SUB), :]


def kernel(
    streams_hbm, filter_ref, rate_ref, residue_ref, gain_ref, grad_hbm,
    output_hbm, grads_hbm,
    xin, gin, obuf, gbuf, s_ref, w_ref, r_ref, sc_ref, rt_ref, q_ref, k_ref, v_ref, u_ref, og_ref, sg_ref, y_ref, m_ref,
    lg_ref, qg_ref, part_ref, inv_ref, cw_ref, rate4, pow_ref,
    ebuf_f, erecv_f, pbuf_f, irecv_f, rbuf_f, rrecv_f,
    ebuf_b, erecv_b, pbuf_b, irecv_b, rbuf_b, rrecv_b,
    sums, sums_recv,
    in_sem, out_sem, halo_send, halo_recv, up_send, up_recv, down_send, down_recv, x_send, x_recv, y_send, y_recv,
):
    ctx = lax.axis_index("ctx")
    tp = lax.axis_index("tp")
    place = lax.rem(ctx, ROW_DEVICES)
    row = lax.div(ctx, ROW_DEVICES)
    ctx_count = ROW_DEVICES * X_COUNT
    next_ctx = lax.rem(ctx + 1, ctx_count)
    prev_ctx = lax.rem(ctx + ctx_count - 1, ctx_count)

    load_x = pltpu.make_async_copy(streams_hbm, xin, in_sem.at[0])
    load_g = pltpu.make_async_copy(grad_hbm, gin, in_sem.at[1])
    load_x.start()
    load_g.start()

    barrier = pltpu.get_barrier_semaphore()

    def greet_ctx(peer):
        pl.semaphore_signal(barrier, inc=1, device_id={"ctx": peer}, device_id_type=MESH)

    greet_ctx(next_ctx)
    greet_ctx(prev_ctx)

    @pl.loop(1, ROW_DEVICES)
    def _(i):
        greet_ctx(row * ROW_DEVICES + lax.rem(place + i, ROW_DEVICES))

    @pl.loop(1, X_COUNT)
    def _(i):
        greet_ctx(lax.rem(row + i, X_COUNT) * ROW_DEVICES + place)

    @pl.loop(1, 8)
    def _(i):
        pl.semaphore_signal(barrier, inc=1, device_id={"tp": lax.rem(tp + i, 8)}, device_id_type=MESH)

    for half in range(2):
        for tile in range(TILES):
            lanes = slice(tile * LANES, (tile + 1) * LANES)
            rate = rate_ref[half * 8 : half * 8 + 8, lanes]
            residue = residue_ref[half * 8 : half * 8 + 8, lanes]
            spread(rt_ref, half * 8, tile, rate)
            spread(r_ref, half * 8, tile, jnp.exp(-rate))
            spread(sc_ref, half * 8, tile, residue * jnp.sqrt(2.0 * rate))
    groups = filter_ref.shape[2]
    spreader = (
        lax.broadcasted_iota(jnp.int32, (groups, TILES * LANES), 1) // GROUP
        == lax.broadcasted_iota(jnp.int32, (groups, TILES * LANES), 0)
    ).astype(F32)
    for s in range(3):
        taps = lax.dot_general(
            filter_ref[s].astype(F32), spreader, (((1,), (0,)), ((), ())), precision=lax.Precision.HIGHEST,
            preferred_element_type=F32,
        )
        for tile in range(TILES):
            spread(w_ref.at[s], 0, tile, taps[:, tile * LANES : (tile + 1) * LANES])
    for mode in range(MODES):
        rates = rt_ref[mode * SUB : mode * SUB + SUB, :]
        rate4[2 * mode] = rates[0:4]
        rate4[2 * mode + 1] = rates[4:8]
    own_rate = rate4[place] * float(ROWS)

    @pl.loop(0, ROW_DEVICES + 1)
    def _(i):
        pow_ref[i] = jnp.exp(-own_rate * i.astype(F32))

    decay = rows_of(r_ref, 0, MODES)

    load_x.wait()

    @pl.loop(0, ROWS // 16)
    def _(b):
        for s in range(3):
            for tile in range(TILES):
                value = xin[s, pl.ds(b * 16, 16), tile * LANES : (tile + 1) * LANES].astype(F32)
                spread(s_ref.at[s], HALO + b * 16, tile, value)

    load_g.wait()
    gain = gain_ref[...]

    @pl.loop(0, ROWS // 16)
    def _(b):
        for tile in range(TILES):
            value = gin[pl.ds(b * 16, 16), tile * LANES : (tile + 1) * LANES].astype(F32)
            spread(og_ref, b * 16, tile, value)

    def short(target, s, start):
        window = rows_of(s_ref.at[s], start + HALO - (TAPS - 1), 8 + TAPS - 1)
        total = rows_of(w_ref.at[s], 0, 1) * window[TAPS - 1 : TAPS - 1 + 8]
        for tap in range(1, TAPS):
            total = total + rows_of(w_ref.at[s], tap, 1) * window[TAPS - 1 - tap : TAPS - 1 - tap + 8]
        if target is not None:
            put_rows(target, start, total)
        return total

    def gated(start):
        keys = short(k_ref, 1, start)
        values = short(v_ref, 2, start)
        u = keys * values
        put_rows(u_ref, start, u)
        return u

    def absorb(state, u):
        for i in range(8):
            state = decay * state + u[i][None]
        return state

    zero_state = jnp.zeros((MODES, SUB, LANES), F32)

    @pl.loop(1, ROWS // 8)
    def _(b):
        gated(b * 8)

    main_end = lax.fori_loop(1, ROWS // 8, lambda b, state: absorb(state, rows_of(u_ref, b * 8, 8)), zero_state)

    pl.semaphore_wait(barrier, 2 + (ROW_DEVICES - 1) + (X_COUNT - 1) + 7)

    def forward_halo(s):
        return pltpu.make_async_remote_copy(
            src_ref=s_ref.at[s, pl.ds((HALO + ROWS - 6) * SUB, 6 * SUB), :],
            dst_ref=s_ref.at[s, pl.ds((HALO - 6) * SUB, 6 * SUB), :],
            send_sem=halo_send.at[s], recv_sem=halo_recv.at[s],
            device_id={"ctx": next_ctx}, device_id_type=MESH,
        )

    def backward_halo(s):
        if s < 3:
            source = s_ref.at[s, pl.ds(HALO * SUB, EXT * SUB), :]
            target = s_ref.at[s, pl.ds((HALO + ROWS) * SUB, EXT * SUB), :]
        else:
            source = og_ref.at[pl.ds(0, EXT * SUB), :]
            target = og_ref.at[pl.ds(ROWS * SUB, EXT * SUB), :]
        return pltpu.make_async_remote_copy(
            src_ref=source, dst_ref=target, send_sem=halo_send.at[3 + s], recv_sem=halo_recv.at[3 + s],
            device_id={"ctx": prev_ctx}, device_id_type=MESH,
        )

    for s in range(3):
        forward_halo(s).start()
    for s in range(4):
        backward_halo(s).start()

    first_device = ctx == 0
    for s in range(3):
        forward_halo(s).wait_recv()
        halo_rows = s_ref[s, pl.ds((HALO - 6) * SUB, 6 * SUB), :]
        s_ref[s, pl.ds((HALO - 6) * SUB, 6 * SUB), :] = jnp.where(first_device, jnp.zeros_like(halo_rows), halo_rows)
    head_end = absorb(zero_state, gated(0))
    head_decay = jnp.exp(rows_of(rt_ref, 0, MODES) * (-float(ROWS - 8)))
    local_end = main_end + head_decay * head_end

    def halves(target, value):
        for mode in range(MODES):
            target[2 * mode] = value[mode, 0:4]
            target[2 * mode + 1] = value[mode, 4:8]

    def exchange(source, target, send_sem, recv_sem, i):
        peer = lax.rem(place + i, ROW_DEVICES)
        return pltpu.make_async_remote_copy(
            src_ref=source.at[peer], dst_ref=target.at[place], send_sem=send_sem.at[i], recv_sem=recv_sem.at[i],
            device_id={"ctx": row * ROW_DEVICES + peer}, device_id_type=MESH,
        )

    def exchange_start(source, target, send_sem, recv_sem):
        @pl.loop(1, ROW_DEVICES)
        def _(i):
            exchange(source, target, send_sem, recv_sem, i).start()

        target[place] = source[place]

    def exchange_wait(source, target, send_sem, recv_sem):
        @pl.loop(1, ROW_DEVICES)
        def _(i):
            exchange(source, target, send_sem, recv_sem, i).wait()

    def x_copy(source, target, which, i):
        peer = lax.rem(row + i, X_COUNT)
        return pltpu.make_async_remote_copy(
            src_ref=source, dst_ref=target.at[row], send_sem=x_send.at[which, i], recv_sem=x_recv.at[which, i],
            device_id={"ctx": peer * ROW_DEVICES + place}, device_id_type=MESH,
        )

    def reduce_states(erecv, pbuf, rbuf, rrecv, which):
        reverse = which == 1
        own_decay = pow_ref[1]

        def step(i, total):
            j = ROW_DEVICES - 1 - i if reverse else i
            pbuf[j] = total
            return own_decay * total + erecv[j]

        total = lax.fori_loop(0, ROW_DEVICES, step, jnp.zeros((4, LANES), F32))
        rbuf[...] = total
        for i in range(1, X_COUNT):
            x_copy(rbuf, rrecv, which, i).start()
        rrecv[row] = total
        for i in range(1, X_COUNT):
            x_copy(rbuf, rrecv, which, i).wait()
        row_decay = pow_ref[ROW_DEVICES]
        entering = jnp.zeros((4, LANES), F32)
        for i in range(X_COUNT):
            j = X_COUNT - 1 - i if reverse else i
            before = j > row if reverse else j < row
            entering = jnp.where(before, row_decay * entering + rrecv[j], entering)

        @pl.loop(0, ROW_DEVICES)
        def _(i):
            j = ROW_DEVICES - 1 - i if reverse else i
            pbuf[j] = pbuf[j] + pow_ref[i] * entering

    def full_states(source):
        return jnp.stack(
            [jnp.concatenate([source[2 * mode], source[2 * mode + 1]], axis=0) for mode in range(MODES)], axis=0
        )

    halves(ebuf_f, local_end)
    exchange_start(ebuf_f, erecv_f, up_send.at[0], up_recv.at[0])

    scale = rows_of(sc_ref, 0, MODES)

    for s in range(4):
        backward_halo(s).wait_recv()
    gated(ROWS)

    @pl.loop(0, BLOCKS)
    def _(b):
        short(q_ref, 0, b * 8)
        put_rows(sg_ref, b * 8, rows_of(og_ref, b * 8, 8) * gain[None])

    def local_rows(b, state):
        u = rows_of(u_ref, b * 8, 8)
        for i in range(8):
            state = decay * state + u[i][None]
            put_rows(y_ref, b * 8 + i, jnp.sum(scale * state, axis=0, keepdims=True))
        return state

    exchange_wait(ebuf_f, erecv_f, up_send.at[0], up_recv.at[0])
    reduce_states(erecv_f, pbuf_f, rbuf_f, rrecv_f, 0)
    exchange_start(pbuf_f, irecv_f, down_send.at[0], down_recv.at[0])
    lax.fori_loop(0, BLOCKS, local_rows, zero_state)
    part_ref[...] = jnp.zeros_like(part_ref)
    exchange_wait(pbuf_f, irecv_f, down_send.at[0], down_recv.at[0])

    def carried_rows(b, moving):
        local = rows_of(y_ref, b * 8, 8)
        rows = []
        for i in range(8):
            moving = moving * decay
            rows.append(local[i] + jnp.sum(moving, axis=0))
        long_conv = jnp.stack(rows, axis=0)
        put_rows(y_ref, b * 8, long_conv)
        modulated = rows_of(q_ref, b * 8, 8) * long_conv
        put_rows(m_ref, b * 8, modulated)
        part_ref[pl.ds(pl.multiple_of(b * 8, 8), 8), :] = jnp.sum(modulated * modulated, axis=1)
        part_ref[pl.ds(pl.multiple_of(256 + b * 8, 8), 8), :] = jnp.sum(
            modulated * rows_of(sg_ref, b * 8, 8), axis=1
        )
        return moving

    lax.fori_loop(0, BLOCKS, carried_rows, scale * full_states(irecv_f))
    totals = lax.dot_general(
        jnp.ones((SUB, LANES), F32), part_ref[...], (((1,), (1,)), ((), ())), precision=lax.Precision.HIGHEST,
        preferred_element_type=F32,
    )
    for i in range(4):
        sums[i : i + 1, :] = totals[0:1, i * LANES : (i + 1) * LANES]

    def y_copy(i):
        peer = lax.rem(tp + i, 8)
        return pltpu.make_async_remote_copy(
            src_ref=sums, dst_ref=sums_recv.at[tp], send_sem=y_send.at[i], recv_sem=y_recv.at[i],
            device_id={"tp": peer}, device_id_type=MESH,
        )

    for i in range(1, 8):
        y_copy(i).start()
    sums_recv[tp] = sums[...]
    for i in range(1, 8):
        y_copy(i).wait()
    summed = jnp.sum(sums_recv[...], axis=0)
    width = float(8 * TILES * LANES)
    inverse = lax.rsqrt(summed[0:2] / width + EPSILON)
    cross = inverse * inverse * inverse * (summed[2:4] / width)
    last_device = ctx == ctx_count - 1
    for target, value in ((inv_ref, inverse), (cw_ref, cross)):
        target[0:ROWS, :] = jnp.transpose(jnp.broadcast_to(value[0:1, :], (LANES, LANES)))
        tail = jnp.transpose(jnp.broadcast_to(value[1:2, :], (LANES, LANES)))[0:EXT, :]
        target[ROWS : ROWS + EXT, :] = jnp.where(last_device, jnp.zeros_like(tail), tail)

    def mixed_rows(b, state):
        start = b * 8
        grad = rows_of(sg_ref, start, 8)
        modulated = rows_of(m_ref, start, 8)
        inverse_rows = inv_ref[pl.ds(pl.multiple_of(start, 8), 8), :].reshape(8, 1, LANES)
        cross_rows = cw_ref[pl.ds(pl.multiple_of(start, 8), 8), :].reshape(8, 1, LANES)
        mixed = inverse_rows * grad - modulated * cross_rows
        put_rows(qg_ref, start, mixed * rows_of(y_ref, start, 8))
        long_grad = mixed * rows_of(q_ref, start, 8)
        put_rows(lg_ref, start, long_grad)
        for i in range(7, -1, -1):
            state = decay * state + long_grad[i][None]
        return state

    adjoint_end = lax.fori_loop(0, BLOCKS - 1, lambda b, state: mixed_rows(BLOCKS - 1 - b, state), zero_state)
    halves(ebuf_b, adjoint_end)
    exchange_start(ebuf_b, erecv_b, up_send.at[1], up_recv.at[1])

    mixed_rows(0, zero_state)

    def round_rows(source, target, start):
        for tile in range(TILES):
            target[pl.ds(pl.multiple_of(start, 16), 16), tile * LANES : (tile + 1) * LANES] = gathered(
                source, start, 16, tile
            ).astype(BF16)

    @pl.loop(0, ROWS // 8)
    def _(b):
        inverse_rows = inv_ref[pl.ds(pl.multiple_of(b * 8, 8), 8), :].reshape(8, 1, LANES)
        put_rows(m_ref, b * 8, gain[None] * rows_of(m_ref, b * 8, 8) * inverse_rows)

    @pl.loop(0, ROWS // 16)
    def _(b):
        round_rows(m_ref, obuf, b * 16)

    store_output = pltpu.make_async_copy(obuf, output_hbm, out_sem.at[3])
    store_output.start()

    def anticausal(source, s, start):
        window = rows_of(source, start, 8 + TAPS - 1)
        total = rows_of(w_ref.at[s], 0, 1) * window[0:8]
        for tap in range(1, TAPS):
            total = total + rows_of(w_ref.at[s], tap, 1) * window[tap : tap + 8]
        return total

    exchange_wait(ebuf_b, erecv_b, up_send.at[1], up_recv.at[1])
    reduce_states(erecv_b, pbuf_b, rbuf_b, rrecv_b, 1)
    exchange_start(pbuf_b, irecv_b, down_send.at[1], down_recv.at[1])

    @pl.loop(0, ROWS // 8)
    def _(b):
        put_rows(m_ref, b * 8, anticausal(qg_ref, 0, b * 8))

    @pl.loop(0, ROWS // 16)
    def _(b):
        round_rows(m_ref, gbuf.at[0], b * 16)

    def store_grad(s):
        return pltpu.make_async_copy(gbuf.at[s], grads_hbm.at[s], out_sem.at[s])

    store_grad(0).start()

    def local_back(b, state):
        start = (BLOCKS - 1 - b) * 8
        long_grad = rows_of(lg_ref, start, 8)
        for i in range(7, -1, -1):
            state = decay * state + long_grad[i][None]
            put_rows(y_ref, start + i, jnp.sum(scale * state, axis=0, keepdims=True))
        return state

    lax.fori_loop(0, BLOCKS, local_back, zero_state)
    exchange_wait(pbuf_b, irecv_b, down_send.at[1], down_recv.at[1])

    def carried_back(b, moving):
        start = (BLOCKS - 1 - b) * 8
        local = rows_of(y_ref, start, 8)
        rows = [None] * 8
        for i in range(7, -1, -1):
            moving = moving * decay
            rows[i] = local[i] + jnp.sum(moving, axis=0)
        gated_grad = jnp.stack(rows, axis=0)
        put_rows(lg_ref, start, gated_grad * rows_of(v_ref, start, 8))
        put_rows(qg_ref, start, gated_grad * rows_of(k_ref, start, 8))
        return moving

    lax.fori_loop(0, BLOCKS, carried_back, scale * full_states(irecv_b))
    for s, source, target in ((1, lg_ref, y_ref), (2, qg_ref, m_ref)):

        @pl.loop(0, ROWS // 8)
        def _(b):
            put_rows(target, b * 8, anticausal(source, s, b * 8))

        @pl.loop(0, ROWS // 16)
        def _(b):
            round_rows(target, gbuf.at[s], b * 16)

        store_grad(s).start()
    for s in range(3):
        forward_halo(s).wait_send()
    for s in range(4):
        backward_halo(s).wait_send()
    store_output.wait()
    for s in range(3):
        store_grad(s).wait()


def on_device(streams, short_filter, decay_rate, residue, norm_gain, out_grad):
    positions = ROWS + EXT
    tiles = lambda count: pltpu.VMEM((count * SUB, LANES), F32)
    states = lambda: [
        pltpu.VMEM((ROW_DEVICES, 4, LANES), F32),
        pltpu.VMEM((ROW_DEVICES, 4, LANES), F32),
        pltpu.VMEM((ROW_DEVICES, 4, LANES), F32),
        pltpu.VMEM((ROW_DEVICES, 4, LANES), F32),
        pltpu.VMEM((4, LANES), F32),
        pltpu.VMEM((X_COUNT, 4, LANES), F32),
    ]
    scratch = [
        pltpu.VMEM(streams.shape, BF16),
        pltpu.VMEM(out_grad.shape, BF16),
        pltpu.VMEM(out_grad.shape, BF16),
        pltpu.VMEM(streams.shape, BF16),
        pltpu.VMEM((3, (HALO + positions) * SUB, LANES), F32),
        pltpu.VMEM((3, 8 * SUB, LANES), F32),
        tiles(MODES),
        tiles(MODES),
        tiles(MODES),
        *[tiles(positions) for _ in range(10)],
        pltpu.VMEM((512, LANES), F32),
        pltpu.VMEM((positions, LANES), F32),
        pltpu.VMEM((positions, LANES), F32),
        pltpu.VMEM((ROW_DEVICES, 4, LANES), F32),
        pltpu.VMEM((ROW_DEVICES + 1, 4, LANES), F32),
        *states(),
        *states(),
        pltpu.VMEM((4, LANES), F32),
        pltpu.VMEM((8, 4, LANES), F32),
        pltpu.SemaphoreType.DMA((2,)),
        pltpu.SemaphoreType.DMA((4,)),
        pltpu.SemaphoreType.DMA((7,)),
        pltpu.SemaphoreType.DMA((7,)),
        pltpu.SemaphoreType.DMA((2, ROW_DEVICES)),
        pltpu.SemaphoreType.DMA((2, ROW_DEVICES)),
        pltpu.SemaphoreType.DMA((2, ROW_DEVICES)),
        pltpu.SemaphoreType.DMA((2, ROW_DEVICES)),
        pltpu.SemaphoreType.DMA((2, X_COUNT)),
        pltpu.SemaphoreType.DMA((2, X_COUNT)),
        pltpu.SemaphoreType.DMA((8,)),
        pltpu.SemaphoreType.DMA((8,)),
    ]
    vmem = pl.BlockSpec(memory_space=pltpu.VMEM)
    anywhere = pl.BlockSpec(memory_space=pl.ANY)
    taps = jnp.pad(jnp.transpose(short_filter, (0, 2, 1)), ((0, 0), (0, 1), (0, 0)))
    return pl.pallas_call(
        kernel,
        out_shape=(
            jax.ShapeDtypeStruct(out_grad.shape, BF16),
            jax.ShapeDtypeStruct(streams.shape, BF16),
        ),
        in_specs=[anywhere, vmem, vmem, vmem, vmem, anywhere],
        out_specs=(anywhere, anywhere),
        scratch_shapes=scratch,
        compiler_params=pltpu.CompilerParams(collective_id=0, has_side_effects=True, vmem_limit_bytes=48 * 2**20),
        name="hyena",
    )(streams, taps, decay_rate, residue, norm_gain.reshape(SUB, LANES), out_grad)


def solution(mesh):
    return jax.shard_map(
        on_device,
        mesh=mesh,
        in_specs=(
            P(None, "ctx", "tp"),
            P(None, "tp", None),
            P(None, "tp"),
            P(None, "tp"),
            P("tp"),
            P("ctx", "tp"),
        ),
        out_specs=(P("ctx", "tp"), P(None, "ctx", "tp")),
        check_vma=False,
    )
```

time: 1060 us -> 85.5 us (0.08); the launches traced: 1050 us -> 85.1 us
  waiting for transfers between devices: 418 us -> 0 us
  blocking collectives: 268 us -> 0 us
  other arithmetic: 165 us -> 0 us
  loops' own time: 83 us -> 0 us
  local copies, waits for them, and re-layouts: 88.9 us -> 6.05 us
  Pallas kernels: 0 us -> 78.4 us
  between operations: 14.4 us -> 0.65 us
    all_gather x2 -> x0, waiting for transfers between devices: 413 us -> none  [carried_in(): gathered = jax.tree.map(lambda a: lax.all_gather(a, axis), part)]
    unnamed x1 -> x0, blocking collectives: 254 us -> none
    add x148 -> x0, other arithmetic: 132 us -> none  [the longest x127 112 us: combine(): reach_decay * earlier_part[1] + later_part[1]]
    another operation x4 -> x0, loops' own time: 83 us -> none  [the longest x2 82.7 us: carried_in(): return lax.fori_loop(0, ahead, one, state)]
    pallas_call x0 -> x1, Pallas kernels: none -> 78.4 us  [on_device(): pl.pallas_call(kernel, out_shape=(jax.ShapeDtypeStruct(out_grad.shape, BF...]
    dynamic_slice x127 -> x0, local copies, waits for them, and re-layouts: 75.9 us -> none  [one(): lax.dynamic_index_in_dim(a, source, 0, False)]
    reduce_sum x6 -> x0, other arithmetic: 15.2 us -> none  [the longest x2 10.3 us: block_terms(): jnp.sum(end_weight[None, :, :, :] * pieces[:, None, :, :], axis=2)]
    psum x1 -> x0, blocking collectives: 14.1 us -> none  [on_device(): lax.psum((jnp.sum(modulated * modulated, axis=1), jnp.sum(scaled_grad * m...]
  transfers between devices with their start and end apart: 4 -> 0, of which waited for: 3 -> 0; matrix products, arithmetic and copies ran while one was open for 1% -> 0% of each run, Pallas kernels for 0% -> 0%
where the time goes in v1:
time: 85.5 us; the launch traced here: 85.1 us
  Pallas kernels  78.4 us (92%)
  local copies, waits for them, and re-layouts  6.05 us (7%)
    pallas_call x1, Pallas kernels, on_device(): pl.pallas_call(kernel, out_shape=(jax.ShapeDtypeStruct(out_grad.shape, BF...  78.4 us
    unnamed x12, local copies, waits for them, and re-layouts  5.35 us

profile of v1, /device:TPU:1, one launch (start us, length us, event | category | flops | bytes accessed | tf_op | source)
XLA Modules:
  0.0 85.1 jit_solution(14351526386236385687)
XLA Ops:
  0.6 0.0 copy-start.4
  0.6 0.7 pad.4.filter_ref
  1.3 0.0 copy-done.4
  1.3 0.0 copy-start
  1.4 1.1 %copy-done = bf16[3,128,1024]{2,1,0:T(8,128)(2,1)S(1)} copy-done((bf16[3,128,1024]{2,1,0:T(8,128)(2,1)S(1)}, bf16[3,128,1024]{2,1,0:T(8,128)(2,1)}, u32[]{:S(2)}) %copy-start) | copy-done | bytes 786456
  2.5 0.0 copy-start.1
  2.5 0.9 %copy-done.1 = bf16[128,1024]{1,0:T(8,128)(2,1)S(1)} copy-done((bf16[128,1024]{1,0:T(8,128)(2,1)S(1)}, bf16[128,1024]{1,0:T(8,128)(2,1)}, u32[]{:S(2)}) %copy-start.1) | copy-done | bytes 262168
  3.4 0.0 copy-start.2
  3.4 0.8 copy-done.2
  4.3 0.0 copy-start.3
  4.3 0.8 copy-done.3
  5.1 78.4 %hyena.1 = (bf16[128,1024]{1,0:T(8,128)(2,1)S(1)}, bf16[3,128,1024]{2,1,0:T(8,128)(2,1)S(1)}) custom-call(bf16[3,128,1024]{2,1,0:T(8,128)(2,1)S(1)} %copy-done, bf16[3,8,64]{2,1,0:T(8,128)(2,1)S(1)} %pad.4.filter_ref, f32[16,1024]{1,0:T(8,128)S(1)} %copy-done.2, f32[16,1024]{1,0:T(8,128)S(1)} %copy-done.3, f32[8,128]{1,0:T(8,128)S(1)} %bitcast.2, ...), custom_call_target="tpu_custom_call" | custom-call | tf_op jit(solution)/shard_map/hyena/pallas_call | solution.py:499
  83.6 0.7 copy.10
  84.3 0.9 %copy.11 = bf16[3,128,1024]{2,1,0:T(8,128)(2,1)} copy(bf16[3,128,1024]{2,1,0:T(8,128)(2,1)S(1)} %get-tuple-element.5) | data formatting | bytes 1572864
Async XLA Ops:
  0.6 0.7 copy-start.4
  1.3 1.1 %copy-start = (bf16[3,128,1024]{2,1,0:T(8,128)(2,1)S(1)}, bf16[3,128,1024]{2,1,0:T(8,128)(2,1)}, u32[]{:S(2)}) copy-start(bf16[3,128,1024]{2,1,0:T(8,128)(2,1)} %streams_hbm.1) | copy-start | bytes 2359300
  2.5 0.9 %copy-start.1 = (bf16[128,1024]{1,0:T(8,128)(2,1)S(1)}, bf16[128,1024]{1,0:T(8,128)(2,1)}, u32[]{:S(2)}) copy-start(bf16[128,1024]{1,0:T(8,128)(2,1)} %grad_hbm.1) | copy-start | bytes 786436
  3.4 0.8 copy-start.2
  4.3 0.8 copy-start.3

commit v2 on v1

--- a/solution.py
+++ b/solution.py
@@ -23,6 +23,7 @@
 ROW_DEVICES = 32
 X_COUNT = 4
 BLOCKS = (ROWS + EXT) // 8
+VMEM_LIMIT = 62 * 2**20
 
 
 def rows_of(ref, start, count):
@@ -48,14 +49,14 @@
 
 
 def kernel(
-    streams_hbm, filter_ref, rate_ref, residue_ref, gain_ref, grad_hbm,
-    output_hbm, grads_hbm,
-    xin, gin, obuf, gbuf, s_ref, w_ref, r_ref, sc_ref, rt_ref, q_ref, k_ref, v_ref, u_ref, og_ref, sg_ref, y_ref, m_ref,
-    lg_ref, qg_ref, part_ref, inv_ref, cw_ref, rate4, pow_ref,
+    streams_hbm, filter_hbm, rate_hbm, residue_hbm, gain_hbm, grad_hbm,
+    obuf, gbuf,
+    filter_ref, rate_ref, residue_ref, gain_ref, xin, gin, s_ref, w_ref, r_ref, sc_ref, rt_ref, q_ref, k_ref, v_ref, u_ref, og_ref, sg_ref, y_ref, m_ref,
+    lg_ref, qg_ref, part_ref, inv_ref, cw_ref, rate4, pow_ref, back_ref,
     ebuf_f, erecv_f, pbuf_f, irecv_f, rbuf_f, rrecv_f,
     ebuf_b, erecv_b, pbuf_b, irecv_b, rbuf_b, rrecv_b,
     sums, sums_recv,
-    in_sem, out_sem, halo_send, halo_recv, up_send, up_recv, down_send, down_recv, x_send, x_recv, y_send, y_recv,
+    in_sem, halo_send, halo_recv, up_send, up_recv, down_send, down_recv, x_send, x_recv, y_send, y_recv,
 ):
     ctx = lax.axis_index("ctx")
     tp = lax.axis_index("tp")
@@ -65,39 +66,53 @@
     next_ctx = lax.rem(ctx + 1, ctx_count)
     prev_ctx = lax.rem(ctx + ctx_count - 1, ctx_count)
 
-    load_x = pltpu.make_async_copy(streams_hbm, xin, in_sem.at[0])
-    load_g = pltpu.make_async_copy(grad_hbm, gin, in_sem.at[1])
-    load_x.start()
-    load_g.start()
+    loads = [
+        pltpu.make_async_copy(source, target, in_sem.at[i])
+        for i, (source, target) in enumerate(
+            (
+                (rate_hbm, rate_ref),
+                (filter_hbm, filter_ref),
+                (streams_hbm.at[1], xin.at[1]),
+                (streams_hbm.at[2], xin.at[2]),
+                (residue_hbm, residue_ref),
+                (streams_hbm.at[0], xin.at[0]),
+                (grad_hbm, gin),
+                (gain_hbm, gain_ref),
+            )
+        )
+    ]
+    for load in loads:
+        load.start()
+
+    def far_first(visit):
+        visit(ROW_DEVICES // 2)
+
+        @pl.loop(1, ROW_DEVICES // 2)
+        def _(i):
+            visit(ROW_DEVICES // 2 - i)
+            visit(ROW_DEVICES // 2 + i)
 
     barrier = pltpu.get_barrier_semaphore()
 
     def greet_ctx(peer):
         pl.semaphore_signal(barrier, inc=1, device_id={"ctx": peer}, device_id_type=MESH)
 
+    far_first(lambda i: greet_ctx(row * ROW_DEVICES + lax.rem(place + i, ROW_DEVICES)))
+    for i in (4, 3, 5, 2, 6, 1, 7):
+        pl.semaphore_signal(barrier, inc=1, device_id={"tp": lax.rem(tp + i, 8)}, device_id_type=MESH)
+    for i in (2, 1, 3):
+        greet_ctx(lax.rem(row + i, X_COUNT) * ROW_DEVICES + place)
     greet_ctx(next_ctx)
     greet_ctx(prev_ctx)
 
-    @pl.loop(1, ROW_DEVICES)
-    def _(i):
-        greet_ctx(row * ROW_DEVICES + lax.rem(place + i, ROW_DEVICES))
-
-    @pl.loop(1, X_COUNT)
-    def _(i):
-        greet_ctx(lax.rem(row + i, X_COUNT) * ROW_DEVICES + place)
-
-    @pl.loop(1, 8)
-    def _(i):
-        pl.semaphore_signal(barrier, inc=1, device_id={"tp": lax.rem(tp + i, 8)}, device_id_type=MESH)
-
+    loads[0].wait()
     for half in range(2):
         for tile in range(TILES):
             lanes = slice(tile * LANES, (tile + 1) * LANES)
             rate = rate_ref[half * 8 : half * 8 + 8, lanes]
-            residue = residue_ref[half * 8 : half * 8 + 8, lanes]
             spread(rt_ref, half * 8, tile, rate)
             spread(r_ref, half * 8, tile, jnp.exp(-rate))
-            spread(sc_ref, half * 8, tile, residue * jnp.sqrt(2.0 * rate))
+    loads[1].wait()
     groups = filter_ref.shape[2]
     spreader = (
         lax.broadcasted_iota(jnp.int32, (groups, TILES * LANES), 1) // GROUP
@@ -110,35 +125,19 @@
         )
         for tile in range(TILES):
             spread(w_ref.at[s], 0, tile, taps[:, tile * LANES : (tile + 1) * LANES])
-    for mode in range(MODES):
-        rates = rt_ref[mode * SUB : mode * SUB + SUB, :]
-        rate4[2 * mode] = rates[0:4]
-        rate4[2 * mode + 1] = rates[4:8]
-    own_rate = rate4[place] * float(ROWS)
-
-    @pl.loop(0, ROW_DEVICES + 1)
-    def _(i):
-        pow_ref[i] = jnp.exp(-own_rate * i.astype(F32))
-
     decay = rows_of(r_ref, 0, MODES)
 
-    load_x.wait()
-
-    @pl.loop(0, ROWS // 16)
-    def _(b):
-        for s in range(3):
+    def to_tiles(s):
+        @pl.loop(0, ROWS // 16)
+        def _(b):
             for tile in range(TILES):
                 value = xin[s, pl.ds(b * 16, 16), tile * LANES : (tile + 1) * LANES].astype(F32)
                 spread(s_ref.at[s], HALO + b * 16, tile, value)
 
-    load_g.wait()
-    gain = gain_ref[...]
-
-    @pl.loop(0, ROWS // 16)
-    def _(b):
-        for tile in range(TILES):
-            value = gin[pl.ds(b * 16, 16), tile * LANES : (tile + 1) * LANES].astype(F32)
-            spread(og_ref, b * 16, tile, value)
+    loads[2].wait()
+    to_tiles(1)
+    loads[3].wait()
+    to_tiles(2)
 
     def short(target, s, start):
         window = rows_of(s_ref.at[s], start + HALO - (TAPS - 1), 8 + TAPS - 1)
@@ -191,18 +190,19 @@
             device_id={"ctx": prev_ctx}, device_id_type=MESH,
         )
 
-    for s in range(3):
+    for s in (1, 2):
         forward_halo(s).start()
-    for s in range(4):
-        backward_halo(s).start()
-
+    head_decay = jnp.exp(rows_of(rt_ref, 0, MODES) * (-float(ROWS - 8)))
     first_device = ctx == 0
-    for s in range(3):
+
+    def receive_head(s):
         forward_halo(s).wait_recv()
         halo_rows = s_ref[s, pl.ds((HALO - 6) * SUB, 6 * SUB), :]
         s_ref[s, pl.ds((HALO - 6) * SUB, 6 * SUB), :] = jnp.where(first_device, jnp.zeros_like(halo_rows), halo_rows)
+
+    for s in (1, 2):
+        receive_head(s)
     head_end = absorb(zero_state, gated(0))
-    head_decay = jnp.exp(rows_of(rt_ref, 0, MODES) * (-float(ROWS - 8)))
     local_end = main_end + head_decay * head_end
 
     def halves(target, value):
@@ -218,16 +218,19 @@
         )
 
     def exchange_start(source, target, send_sem, recv_sem):
-        @pl.loop(1, ROW_DEVICES)
-        def _(i):
-            exchange(source, target, send_sem, recv_sem, i).start()
-
+        far_first(lambda i: exchange(source, target, send_sem, recv_sem, i).start())
         target[place] = source[place]
 
-    def exchange_wait(source, target, send_sem, recv_sem):
-        @pl.loop(1, ROW_DEVICES)
-        def _(i):
+    def exchange_wait(source, target, send_sem, recv_sem, arrived=None):
+        def one(i, total):
             exchange(source, target, send_sem, recv_sem, i).wait()
+            return total if arrived is None else arrived(lax.rem(place - i + ROW_DEVICES, ROW_DEVICES), total)
+
+        total = jnp.zeros((4, LANES), F32) if arrived is None else arrived(place, None)
+        total = lax.fori_loop(
+            1, ROW_DEVICES // 2, lambda i, total: one(ROW_DEVICES - i, one(i, total)), total
+        )
+        return one(ROW_DEVICES // 2, total)
 
     def x_copy(source, target, which, i):
         peer = lax.rem(row + i, X_COUNT)
@@ -236,21 +239,26 @@
             device_id={"ctx": peer * ROW_DEVICES + place}, device_id_type=MESH,
         )
 
-    def reduce_states(erecv, pbuf, rbuf, rrecv, which):
+    def reduce_states(ebuf, erecv, pbuf, rbuf, rrecv, which):
         reverse = which == 1
         own_decay = pow_ref[1]
-
-        def step(i, total):
+        reach = pow_ref if reverse else back_ref
+
+        def arrived(j, total):
+            term = reach[j] * erecv[j]
+            return term if total is None else total + term
+
+        total = exchange_wait(ebuf, erecv, up_send.at[which], up_recv.at[which], arrived)
+        rbuf[...] = total
+        rrecv[row] = total
+        for i in (2, 1, 3):
+            x_copy(rbuf, rrecv, which, i).start()
+        ahead = jnp.zeros((4, LANES), F32)
+        for i in range(ROW_DEVICES):
             j = ROW_DEVICES - 1 - i if reverse else i
-            pbuf[j] = total
-            return own_decay * total + erecv[j]
-
-        total = lax.fori_loop(0, ROW_DEVICES, step, jnp.zeros((4, LANES), F32))
-        rbuf[...] = total
-        for i in range(1, X_COUNT):
-            x_copy(rbuf, rrecv, which, i).start()
-        rrecv[row] = total
-        for i in range(1, X_COUNT):
+            pbuf[j] = ahead
+            ahead = own_decay * ahead + erecv[j]
+        for i in (1, 3, 2):
             x_copy(rbuf, rrecv, which, i).wait()
         row_decay = pow_ref[ROW_DEVICES]
         entering = jnp.zeros((4, LANES), F32)
@@ -258,11 +266,8 @@
             j = X_COUNT - 1 - i if reverse else i
             before = j > row if reverse else j < row
             entering = jnp.where(before, row_decay * entering + rrecv[j], entering)
-
-        @pl.loop(0, ROW_DEVICES)
-        def _(i):
-            j = ROW_DEVICES - 1 - i if reverse else i
-            pbuf[j] = pbuf[j] + pow_ref[i] * entering
+        powers = back_ref[...] if reverse else pow_ref[0:ROW_DEVICES]
+        pbuf[...] = pbuf[...] + powers * entering[None]
 
     def full_states(source):
         return jnp.stack(
@@ -272,8 +277,44 @@
     halves(ebuf_f, local_end)
     exchange_start(ebuf_f, erecv_f, up_send.at[0], up_recv.at[0])
 
+    loads[5].wait()
+    to_tiles(0)
+    forward_halo(0).start()
+    loads[6].wait()
+
+    @pl.loop(0, ROWS // 16)
+    def _(b):
+        for tile in range(TILES):
+            value = gin[pl.ds(b * 16, 16), tile * LANES : (tile + 1) * LANES].astype(F32)
+            spread(og_ref, b * 16, tile, value)
+
+    for s in range(4):
+        backward_halo(s).start()
+    loads[4].wait()
+    for half in range(2):
+        for tile in range(TILES):
+            lanes = slice(tile * LANES, (tile + 1) * LANES)
+            residue = residue_ref[half * 8 : half * 8 + 8, lanes]
+            rate = rate_ref[half * 8 : half * 8 + 8, lanes]
+            spread(sc_ref, half * 8, tile, residue * jnp.sqrt(2.0 * rate))
+    for mode in range(MODES):
+        rates = rt_ref[mode * SUB : mode * SUB + SUB, :]
+        rate4[2 * mode] = rates[0:4]
+        rate4[2 * mode + 1] = rates[4:8]
+    own_rate = rate4[place] * float(ROWS)
+
+    @pl.loop(0, ROW_DEVICES + 1)
+    def _(i):
+        pow_ref[i] = jnp.exp(-own_rate * i.astype(F32))
+
+    @pl.loop(0, ROW_DEVICES)
+    def _(i):
+        back_ref[i] = pow_ref[ROW_DEVICES - 1 - i]
+
+    loads[7].wait()
+    gain = gain_ref[...]
     scale = rows_of(sc_ref, 0, MODES)
-
+    receive_head(0)
     for s in range(4):
         backward_halo(s).wait_recv()
     gated(ROWS)
@@ -290,8 +331,7 @@
             put_rows(y_ref, b * 8 + i, jnp.sum(scale * state, axis=0, keepdims=True))
         return state
 
-    exchange_wait(ebuf_f, erecv_f, up_send.at[0], up_recv.at[0])
-    reduce_states(erecv_f, pbuf_f, rbuf_f, rrecv_f, 0)
+    reduce_states(ebuf_f, erecv_f, pbuf_f, rbuf_f, rrecv_f, 0)
     exchange_start(pbuf_f, irecv_f, down_send.at[0], down_recv.at[0])
     lax.fori_loop(0, BLOCKS, local_rows, zero_state)
     part_ref[...] = jnp.zeros_like(part_ref)
@@ -328,10 +368,10 @@
             device_id={"tp": peer}, device_id_type=MESH,
         )
 
-    for i in range(1, 8):
+    for i in (4, 3, 5, 2, 6, 1, 7):
         y_copy(i).start()
     sums_recv[tp] = sums[...]
-    for i in range(1, 8):
+    for i in (1, 7, 2, 6, 3, 5, 4):
         y_copy(i).wait()
     summed = jnp.sum(sums_recv[...], axis=0)
     width = float(8 * TILES * LANES)
@@ -378,9 +418,6 @@
     def _(b):
         round_rows(m_ref, obuf, b * 16)
 
-    store_output = pltpu.make_async_copy(obuf, output_hbm, out_sem.at[3])
-    store_output.start()
-
     def anticausal(source, s, start):
         window = rows_of(source, start, 8 + TAPS - 1)
         total = rows_of(w_ref.at[s], 0, 1) * window[0:8]
@@ -388,8 +425,7 @@
             total = total + rows_of(w_ref.at[s], tap, 1) * window[tap : tap + 8]
         return total
 
-    exchange_wait(ebuf_b, erecv_b, up_send.at[1], up_recv.at[1])
-    reduce_states(erecv_b, pbuf_b, rbuf_b, rrecv_b, 1)
+    reduce_states(ebuf_b, erecv_b, pbuf_b, rbuf_b, rrecv_b, 1)
     exchange_start(pbuf_b, irecv_b, down_send.at[1], down_recv.at[1])
 
     @pl.loop(0, ROWS // 8)
@@ -399,11 +435,6 @@
     @pl.loop(0, ROWS // 16)
     def _(b):
         round_rows(m_ref, gbuf.at[0], b * 16)
-
-    def store_grad(s):
-        return pltpu.make_async_copy(gbuf.at[s], grads_hbm.at[s], out_sem.at[s])
-
-    store_grad(0).start()
 
     def local_back(b, state):
         start = (BLOCKS - 1 - b) * 8
@@ -439,14 +470,19 @@
         def _(b):
             round_rows(target, gbuf.at[s], b * 16)
 
-        store_grad(s).start()
     for s in range(3):
         forward_halo(s).wait_send()
     for s in range(4):
         backward_halo(s).wait_send()
-    store_output.wait()
-    for s in range(3):
-        store_grad(s).wait()
+
+
+def hand_out(output_ref, grads_ref, output_hbm, grads_hbm, sem):
+    copies = [pltpu.make_async_copy(grads_ref.at[s], grads_hbm.at[s], sem.at[s]) for s in range(3)]
+    copies.append(pltpu.make_async_copy(output_ref, output_hbm, sem.at[3]))
+    for copy in copies:
+        copy.start()
+    for copy in copies:
+        copy.wait()
 
 
 def on_device(streams, short_filter, decay_rate, residue, norm_gain, out_grad):
@@ -461,10 +497,12 @@
         pltpu.VMEM((X_COUNT, 4, LANES), F32),
     ]
     scratch = [
+        pltpu.VMEM((3, TAPS, short_filter.shape[1]), BF16),
+        pltpu.VMEM(decay_rate.shape, F32),
+        pltpu.VMEM(residue.shape, F32),
+        pltpu.VMEM((SUB, LANES), F32),
         pltpu.VMEM(streams.shape, BF16),
         pltpu.VMEM(out_grad.shape, BF16),
-        pltpu.VMEM(out_grad.shape, BF16),
-        pltpu.VMEM(streams.shape, BF16),
         pltpu.VMEM((3, (HALO + positions) * SUB, LANES), F32),
         pltpu.VMEM((3, 8 * SUB, LANES), F32),
         tiles(MODES),
@@ -476,12 +514,12 @@
         pltpu.VMEM((positions, LANES), F32),
         pltpu.VMEM((ROW_DEVICES, 4, LANES), F32),
         pltpu.VMEM((ROW_DEVICES + 1, 4, LANES), F32),
+        pltpu.VMEM((ROW_DEVICES, 4, LANES), F32),
         *states(),
         *states(),
         pltpu.VMEM((4, LANES), F32),
         pltpu.VMEM((8, 4, LANES), F32),
-        pltpu.SemaphoreType.DMA((2,)),
-        pltpu.SemaphoreType.DMA((4,)),
+        pltpu.SemaphoreType.DMA((8,)),
         pltpu.SemaphoreType.DMA((7,)),
         pltpu.SemaphoreType.DMA((7,)),
         pltpu.SemaphoreType.DMA((2, ROW_DEVICES)),
@@ -493,21 +531,28 @@
         pltpu.SemaphoreType.DMA((8,)),
         pltpu.SemaphoreType.DMA((8,)),
     ]
-    vmem = pl.BlockSpec(memory_space=pltpu.VMEM)
+    stay = pl.BlockSpec(memory_space=pltpu.HBM)
     anywhere = pl.BlockSpec(memory_space=pl.ANY)
-    taps = jnp.pad(jnp.transpose(short_filter, (0, 2, 1)), ((0, 0), (0, 1), (0, 0)))
-    return pl.pallas_call(
+    taps = jnp.transpose(short_filter, (0, 2, 1))
+    shapes = (jax.ShapeDtypeStruct(out_grad.shape, BF16), jax.ShapeDtypeStruct(streams.shape, BF16))
+    output, grads = pl.pallas_call(
         kernel,
-        out_shape=(
-            jax.ShapeDtypeStruct(out_grad.shape, BF16),
-            jax.ShapeDtypeStruct(streams.shape, BF16),
-        ),
-        in_specs=[anywhere, vmem, vmem, vmem, vmem, anywhere],
-        out_specs=(anywhere, anywhere),
+        out_shape=tuple(pltpu.VMEM(shape.shape, BF16) for shape in shapes),
+        in_specs=[stay] * 6,
+        out_specs=(pl.BlockSpec(memory_space=pltpu.VMEM),) * 2,
         scratch_shapes=scratch,
-        compiler_params=pltpu.CompilerParams(collective_id=0, has_side_effects=True, vmem_limit_bytes=48 * 2**20),
+        compiler_params=pltpu.CompilerParams(collective_id=0, has_side_effects=True, vmem_limit_bytes=VMEM_LIMIT),
         name="hyena",
     )(streams, taps, decay_rate, residue, norm_gain.reshape(SUB, LANES), out_grad)
+    return pl.pallas_call(
+        hand_out,
+        out_shape=shapes,
+        in_specs=[anywhere] * 2,
+        out_specs=(anywhere, anywhere),
+        scratch_shapes=[pltpu.SemaphoreType.DMA((4,))],
+        compiler_params=pltpu.CompilerParams(vmem_limit_bytes=2**20),
+        name="hand_out",
+    )(output, grads)
 
 
 def solution(mesh):

time: 85.5 us -> 75 us (0.88)
  local copies, waits for them, and re-layouts: 6.05 us -> 0 us
  Pallas kernels: 78.4 us -> 74.2 us
    unnamed x12 -> x0, local copies, waits for them, and re-layouts: 5.35 us -> none
    pallas_call x1 -> x2, Pallas kernels: 78.4 us -> 74.2 us  [the longest x1 73.2 us: on_device(): pl.pallas_call(kernel, out_shape=tuple((pltpu.VMEM(shape.shape, BF16) for...]
where the time goes in v2:
time: 75 us; the launch traced here: 74.8 us
  Pallas kernels  74.2 us (99%)
    pallas_call x1, Pallas kernels, on_device(): pl.pallas_call(kernel, out_shape=tuple((pltpu.VMEM(shape.shape, BF16) for...  73.2 us

profile of v2, /device:TPU:1, one launch (start us, length us, event | category | flops | bytes accessed | tf_op | source)
XLA Modules:
  0.0 74.8 jit_solution(4500372365372807171)
XLA Ops:
  0.6 73.2 %hyena.1 = (bf16[128,1024]{1,0:T(8,128)(2,1)S(1)}, bf16[3,128,1024]{2,1,0:T(8,128)(2,1)S(1)}) custom-call(bf16[3,128,1024]{2,1,0:T(8,128)(2,1)} %streams_hbm.1, bf16[3,7,64]{2,1,0:T(8,128)(2,1)} %bitcast.2, f32[16,1024]{1,0:T(8,128)} %rate_hbm.1, f32[16,1024]{1,0:T(8,128)} %residue_hbm.1, f32[8,128]{1,0:T(8,128)} %bitcast.3, bf16[128,1024]{1,0:T(8,128)(2,1)} %grad_hbm.1), custom_call_target="tpu_custom_call" | custom-call | tf_op jit(solution)/shard_map/hyena/pallas_call | solution.py:538
  73.8 1.0 %hand_out.1 = (bf16[128,1024]{1,0:T(8,128)(2,1)}, bf16[3,128,1024]{2,1,0:T(8,128)(2,1)}) custom-call(bf16[128,1024]{1,0:T(8,128)(2,1)S(1)} %get-tuple-element.4.output_ref, bf16[3,128,1024]{2,1,0:T(8,128)(2,1)S(1)} %get-tuple-element.5.grads_ref), custom_call_target="tpu_custom_call" | custom-call | tf_op jit(solution)/shard_map/hand_out/pallas_call | solution.py:547
